TPU v7x, 512 devices: a whole 4x8x8 slice. The times are simulated.
512 devices in a mesh: node: 64 (over y, z_lo, core), local: 8 (over z_hi, x).
Axes of the slice: x: 4, y: 8, z: 8 (z_hi: 2, z_lo: 4; z = z_hi * 4 + z_lo), core: 2. Of those that a mesh axis runs over, the one named last changes fastest.
Arguments:
- hidden_acts: bfloat16 [65536, 1024], P(('node', 'local')), may hold values from -6 to 6
- out_grad: bfloat16 [65536, 4096], P(('node', 'local')), may hold values from -6 to 6
- weight: bfloat16 [32768, 4096], P('node', 'local'), may hold values from -0.1875 to 0.1875
- first_moment: bfloat16 [32768, 4096], P('node', 'local'), may hold values from -6 to 6
- second_moment: bfloat16 [32768, 4096], P('node', 'local'), may hold values from 0.5 to 8
- holder_expert: int32 [32], replicated, may hold values from 0 to 31
- new_source: int32 [32], replicated, may hold values from 0 to 31, as said below
- live_blocks: int32 [64, 8], P('node', 'local'), may hold values from 1 to 4, as said below
Outputs:
- next_weight: bfloat16 [32768, 4096], P('node', 'local')
- next_first: bfloat16 [32768, 4096], P('node', 'local')
- next_second: bfloat16 [32768, 4096], P('node', 'local')
- hidden_back: bfloat16 [65536, 1024], P(('node', 'local'))
Inputs may be any that keep to these rules, and one draw needn't show every extreme that they name: `new_source`: each entry names a copy. The live rows of a device are its first 32 * live_blocks rows.
All inputs are finite; a program needn't handle non-finite values.
Results may differ from a plain program's by a relative error of at most 0.001.
Values may be sent and summed in bfloat16 or wider, within the bound.
A program may use at most 64 MiB of HBM per device.

v0:
```python
import jax
import jax.numpy as jnp
from jax import lax
from jax.sharding import PartitionSpec as P

ROW_BLOCK = 32
beta_one = 0.9
beta_two = 0.95
learn_rate = 0.002
decay_rate = 0.1
adam_eps = 1e-08
step_count = 10.0


def swapped(block, axis, distance):
    count = lax.axis_size(axis)
    route = []
    for low in range(count):
        high = low | 1 << distance
        if high != low and high < count:
            route += [(low, high), (high, low)]
    return lax.ppermute(block, axis, route)


def shortened(array):
    return jax.tree.map(lambda a: a.astype(jnp.bfloat16) if a.dtype == jnp.float32 else a, array)


def adamw_step(gradient, weight, first, second):
    first_new = beta_one * first.astype(jnp.float32) + (1.0 - beta_one) * gradient
    second_new = beta_two * second.astype(jnp.float32) + (1.0 - beta_two) * gradient * gradient
    update = (
        first_new
        / (1.0 - beta_one**step_count)
        / (jnp.sqrt(second_new / (1.0 - beta_two**step_count)) + adam_eps)
    )
    master = weight.astype(jnp.float32)
    weight_new = master - learn_rate * (update + decay_rate * master)
    return (
        weight_new.astype(jnp.bfloat16),
        first_new.astype(jnp.bfloat16),
        second_new.astype(jnp.bfloat16),
    )


def group_total(group_blend, gradient, node_count):
    col_count = gradient.shape[1]
    stacked = gradient.reshape(node_count, -1, col_count)
    return jnp.einsum("kj,jrc->krc", group_blend, stacked, precision=lax.Precision.HIGHEST)


def shards(
    hidden_acts,
    out_grad,
    weight,
    first_moment,
    second_moment,
    holder_expert,
    new_source,
    live_blocks,
):
    tok_rows = out_grad.shape[0]
    half_rows = weight.shape[0]
    row_ids = lax.broadcasted_iota(jnp.int32, (tok_rows, 1), 0)
    live_rows = live_blocks[0, 0] * ROW_BLOCK
    masked = jnp.where(row_ids < live_rows, out_grad, jnp.zeros_like(out_grad))
    columns = lax.all_to_all(masked, "local", split_axis=1, concat_axis=0, tiled=True)
    parity = lax.axis_index("node") % 2
    partner_half = swapped(weight, "node", 0)
    full_weight = jnp.where(
        parity == 0,
        jnp.concatenate([weight, partner_half], axis=0),
        jnp.concatenate([partner_half, weight], axis=0),
    )
    row_part = columns
    grad_whole = lax.dot_general(
        lax.all_gather(hidden_acts, "local", axis=0, tiled=True),
        row_part,
        (((0,), (0,)), ((), ())),
        preferred_element_type=jnp.float32,
    )
    row_part = columns
    hidden_back = lax.psum_scatter(
        lax.dot_general(
            row_part, full_weight, (((1,), (1,)), ((), ())), preferred_element_type=jnp.float32
        ),
        "local",
        scatter_dimension=0,
        tiled=True,
    ).astype(jnp.bfloat16)
    own_part = lax.dynamic_slice_in_dim(grad_whole, parity * half_rows, half_rows, 0)
    other_part = lax.dynamic_slice_in_dim(grad_whole, (1 - parity) * half_rows, half_rows, 0)
    grad_part = own_part + swapped(other_part, "node", 0)
    node_count = lax.axis_size("node")
    node_ids = jnp.arange(node_count, dtype=jnp.int32)
    node_holder = jnp.repeat(holder_expert, 2)
    node_parity = node_ids % 2
    group_blend = (
        (node_holder[:, None] == node_holder[None, :])
        & (node_parity[:, None] == node_parity[None, :])
    ).astype(jnp.float32)
    source_node = 2 * jnp.repeat(new_source, 2) + node_parity
    pieces = lax.all_to_all(grad_part, "node", split_axis=0, concat_axis=0, tiled=True)
    col_count = pieces.shape[1]
    summed = group_total(group_blend, pieces, node_count)
    full_grad = lax.all_to_all(
        summed.reshape(-1, col_count), "node", split_axis=0, concat_axis=0, tiled=True
    )
    weight_new, first_new, second_new = adamw_step(full_grad, weight, first_moment, second_moment)
    pieces = (
        lax.all_to_all(weight_new, "node", split_axis=0, concat_axis=0, tiled=True),
        lax.all_to_all(first_new, "node", split_axis=0, concat_axis=0, tiled=True),
        lax.all_to_all(second_new, "node", split_axis=0, concat_axis=0, tiled=True),
    )
    col_count = pieces[0].shape[1]
    migrated = tuple(
        (
            jnp.take(state.reshape(node_count, -1, col_count), source_node, axis=0).reshape(
                -1, col_count
            )
            for state in pieces
        )
    )
    next_weight, next_first, next_second = jax.tree.map(
        lambda part, own: part.astype(own.dtype),
        lax.all_to_all(shortened(migrated), "node", split_axis=0, concat_axis=0, tiled=True),
        migrated,
    )
    return (next_weight, next_first, next_second, hidden_back)


def solution(mesh):
    return jax.shard_map(
        shards,
        mesh=mesh,
        in_specs=(
            P(("node", "local"), None),
            P(("node", "local"), None),
            P("node", "local"),
            P("node", "local"),
            P("node", "local"),
            P(),
            P(),
            P("node", "local"),
        ),
        out_specs=(
            P("node", "local"),
            P("node", "local"),
            P("node", "local"),
            P(("node", "local"), None),
        ),
        check_vma=False,
    )
```

profile of v0, /device:TPU:1, one launch (start us, length us, event | category | flops | bytes accessed | tf_op | source)
XLA Modules:
  0.0 386.4 jit_solution(8248881727902081018)
XLA Ops:
  8.5 1.6 copy.21
  10.2 1.1 broadcast_select_fusion
  11.2 13.3 %all-to-all-start = ((bf16[128,8,512]{0,2,1:T(8,128)(2,1)}), bf16[128,8,512]{0,2,1:T(8,128)(2,1)S(1)}, u32[]{:S(2)}, u32[]{:S(2)}) async-start(bf16[128,8,512]{0,2,1:T(8,128)(2,1)} %bitcast.2), calls=%async_computation | async-start | bytes 2097152 | tf_op jit(solution)/shard_map/all_to_all | solution.py:67
  24.5 18.6 %all-to-all-done = bf16[128,8,512]{0,2,1:T(8,128)(2,1)S(1)} async-done(((bf16[128,8,512]{0,2,1:T(8,128)(2,1)}), bf16[128,8,512]{0,2,1:T(8,128)(2,1)S(1)}, u32[]{:S(2)}, u32[]{:S(2)}) %all-to-all-start) | async-done | bytes 1048608 | tf_op jit(solution)/shard_map/all_to_all | solution.py:67
  43.7 65.6 %all-gather.2.cloned.1.call-done = bf16[1024,1024]{1,0:T(8,128)(2,1)} async-done(((bf16[128,1024]{1,0:T(8,128)(2,1)}), bf16[1024,1024]{1,0:T(8,128)(2,1)}) %all-gather.2.cloned.1.call-update) | async-done | bytes 2097168 | tf_op jit(solution)/shard_map/all_gather | solution.py:77
  109.3 2.9 fusion.28
  112.1 1.1 dynamic-slice_bitcast_fusion
  113.2 4.1 %collective-permute-start = (f32[512,512]{0,1:T(8,128)}, f32[512,512]{0,1:T(8,128)}, u32[]{:S(2)}, u32[]{:S(2)}) collective-permute-start(f32[512,512]{0,1:T(8,128)} %dynamic-slice_bitcast_fusion), channel_id=1, source_target_pairs={{0,8},{8,0},{16,24},{24,16},{32,40},{40,32},{48,56},{56,48},{64,72... | collective-permute-start | bytes 3145736 | tf_op jit(solution)/shard_map/ppermute | solution.py:22
  117.4 2.6 collective-permute-done
  120.0 2.4 bitcast_add_fusion
  122.4 2.6 copy.23
  125.0 8.1 %all-to-all-start.1 = ((f32[64,8,512]{2,1,0:T(8,128)}), f32[64,8,512]{2,1,0:T(8,128)S(1)}, u32[]{:S(2)}, u32[]{:S(2)}) async-start(f32[64,8,512]{2,1,0:T(8,128)} %bitcast.7), calls=%async_computation.1 | async-start | bytes 2097152 | tf_op jit(solution)/shard_map/all_to_all | solution.py:103
  133.1 2.4 collective-permute-start.1
  135.7 26.0 %all-to-all-done.1 = f32[64,8,512]{2,1,0:T(8,128)S(1)} async-done(((f32[64,8,512]{2,1,0:T(8,128)}), f32[64,8,512]{2,1,0:T(8,128)S(1)}, u32[]{:S(2)}, u32[]{:S(2)}) %all-to-all-start.1) | async-done | bytes 1048608 | tf_op jit(solution)/shard_map/all_to_all | solution.py:103
  161.6 1.3 fusion.11
  162.9 1.6 copy.25
  164.5 6.0 %all-to-all-start.2 = ((f32[64,8,512]{2,1,0:T(8,128)}), f32[64,8,512]{2,1,0:T(8,128)S(1)}, u32[]{:S(2)}, u32[]{:S(2)}) async-start(f32[64,8,512]{2,1,0:T(8,128)} %copy.25), calls=%async_computation.2 | async-start | bytes 2097152 | tf_op jit(solution)/shard_map/all_to_all | solution.py:106
  170.6 4.4 %fusion.4 = f32[1024,1024]{1,0:T(8,128)} fusion(bf16[1024,512]{1,0:T(8,128)(2,1)S(1)} %bitcast.44, bf16[512,512]{1,0:T(8,128)(2,1)} %collective-permute-done.1, bf16[512,512]{1,0:T(8,128)(2,1)S(1)} %copy-done.2, pred[]{:T(512)S(6)} %eq.42), kind=kOutput, calls=%fused_computation.11 | convolution fusion | flops 1078460416 | bytes 6291457 | tf_op jit(solution)/shard_map/dot_general | solution.py:84
  175.0 25.2 %all-to-all-done.2 = f32[64,8,512]{2,1,0:T(8,128)S(1)} async-done(((f32[64,8,512]{2,1,0:T(8,128)}), f32[64,8,512]{2,1,0:T(8,128)S(1)}, u32[]{:S(2)}, u32[]{:S(2)}) %all-to-all-start.2) | async-done | bytes 1048608 | tf_op jit(solution)/shard_map/all_to_all | solution.py:106
  200.2 1.8 fusion.16
  202.0 42.0 %all_to_all.91 = bf16[64,8,512]{2,1,0:T(8,128)(2,1)S(1)} all-to-all(bf16[64,8,512]{2,1,0:T(8,128)(2,1)S(1)} %get-tuple-element.7), channel_id=1, replica_groups=mesh['node'=64,'local'=8] {'node'}, dimensions={0} | all-to-all | bytes 1048576 | tf_op jit(solution)/shard_map/all_to_all | solution.py:113
  244.0 25.3 %all_to_all.92 = bf16[64,8,512]{2,1,0:T(8,128)(2,1)S(1)} all-to-all(bf16[64,8,512]{2,1,0:T(8,128)(2,1)S(1)} %get-tuple-element.8), channel_id=1, replica_groups=mesh['node'=64,'local'=8] {'node'}, dimensions={0} | all-to-all | bytes 1048576 | tf_op jit(solution)/shard_map/all_to_all | solution.py:111
  269.3 16.3 %all-to-all-start.5 = ((bf16[64,8,512]{2,1,0:T(8,128)(2,1)}), bf16[64,8,512]{2,1,0:T(8,128)(2,1)S(1)}, u32[]{:S(2)}, u32[]{:S(2)}) async-start(bf16[64,8,512]{2,1,0:T(8,128)(2,1)} %get-tuple-element.9), calls=%async_computation.5 | async-start | bytes 1048576 | tf_op jit(solution)/shard_map/all_to_all | solution.py:112
  287.1 16.3 %all-to-all-done.5 = bf16[64,8,512]{2,1,0:T(8,128)(2,1)S(1)} async-done(((bf16[64,8,512]{2,1,0:T(8,128)(2,1)}), bf16[64,8,512]{2,1,0:T(8,128)(2,1)S(1)}, u32[]{:S(2)}, u32[]{:S(2)}) %all-to-all-start.5) | async-done | bytes 524320 | tf_op jit(solution)/shard_map/all_to_all | solution.py:112
  303.9 1.0 broadcast_select_fusion.1
  304.9 23.1 %all_to_all.93 = bf16[64,8,512]{2,1,0:T(8,128)(2,1)S(1)} all-to-all(bf16[64,8,512]{2,1,0:T(8,128)(2,1)S(1)} %get-tuple-element.10), channel_id=1, replica_groups=mesh['node'=64,'local'=8] {'node'}, dimensions={0} | all-to-all | bytes 1048576 | tf_op jit(solution)/shard_map/all_to_all | solution.py:126
  328.1 25.8 %all_to_all.94 = bf16[64,8,512]{2,1,0:T(8,128)(2,1)S(1)} all-to-all(bf16[64,8,512]{2,1,0:T(8,128)(2,1)S(1)} %get-tuple-element.11), channel_id=1, replica_groups=mesh['node'=64,'local'=8] {'node'}, dimensions={0} | all-to-all | bytes 1048576 | tf_op jit(solution)/shard_map/all_to_all | solution.py:126
  353.9 5.6 %all-to-all-start.4 = ((bf16[64,8,512]{2,1,0:T(8,128)(2,1)}), bf16[64,8,512]{2,1,0:T(8,128)(2,1)S(1)}, u32[]{:S(2)}, u32[]{:S(2)}) async-start(bf16[64,8,512]{2,1,0:T(8,128)(2,1)} %get-tuple-element.12), calls=%async_computation.4 | async-start | bytes 1048576 | tf_op jit(solution)/shard_map/all_to_all | solution.py:126
  359.5 1.8 convert_element_type.28
  361.3 15.9 %all-to-all-done.4 = bf16[64,8,512]{2,1,0:T(8,128)(2,1)S(1)} async-done(((bf16[64,8,512]{2,1,0:T(8,128)(2,1)}), bf16[64,8,512]{2,1,0:T(8,128)(2,1)S(1)}, u32[]{:S(2)}, u32[]{:S(2)}) %all-to-all-start.4) | async-done | bytes 524320 | tf_op jit(solution)/shard_map/all_to_all | solution.py:126
  377.2 0.8 copy.32
  378.0 0.8 copy.33
  (30 shorter events, 4.3 us)
Async XLA Ops:
  7.2 102.1 %all-gather.2.cloned.1.call-start = ((), (), s32[]{:S(2)}) async-start(), calls=%async_computation.10 | async-start | bytes 2359296 | tf_op jit(solution)/shard_map/all_gather | solution.py:77
  11.2 31.9 %all-to-all-start = ((bf16[128,8,512]{0,2,1:T(8,128)(2,1)}), bf16[128,8,512]{0,2,1:T(8,128)(2,1)S(1)}, u32[]{:S(2)}, u32[]{:S(2)}) async-start(bf16[128,8,512]{0,2,1:T(8,128)(2,1)} %bitcast.2), calls=%async_computation | async-start | bytes 2097152 | tf_op jit(solution)/shard_map/all_to_all | solution.py:67
  113.2 6.8 %collective-permute-start = (f32[512,512]{0,1:T(8,128)}, f32[512,512]{0,1:T(8,128)}, u32[]{:S(2)}, u32[]{:S(2)}) collective-permute-start(f32[512,512]{0,1:T(8,128)} %dynamic-slice_bitcast_fusion), channel_id=1, source_target_pairs={{0,8},{8,0},{16,24},{24,16},{32,40},{40,32},{48,56},{56,48},{64,72... | collective-permute-start | bytes 3145736 | tf_op jit(solution)/shard_map/ppermute | solution.py:22
  122.4 10.7 %copy-start.2 = (bf16[512,512]{1,0:T(8,128)(2,1)S(1)}, bf16[512,512]{1,0:T(8,128)(2,1)}, u32[]{:S(2)}) copy-start(bf16[512,512]{1,0:T(8,128)(2,1)} %param.12) | copy-start | bytes 1572868
  122.4 13.1 %copy-start.3 = (s32[32]{0:T(128)S(1)}, s32[32]{0:T(128)}, u32[]{:S(2)}) copy-start(s32[32]{0:T(128)} %param.15) | copy-start | bytes 388
  125.0 36.7 %all-to-all-start.1 = ((f32[64,8,512]{2,1,0:T(8,128)}), f32[64,8,512]{2,1,0:T(8,128)S(1)}, u32[]{:S(2)}, u32[]{:S(2)}) async-start(f32[64,8,512]{2,1,0:T(8,128)} %bitcast.7), calls=%async_computation.1 | async-start | bytes 2097152 | tf_op jit(solution)/shard_map/all_to_all | solution.py:103
  133.1 37.5 %collective-permute-start.1 = (bf16[512,512]{1,0:T(8,128)(2,1)S(1)}, bf16[512,512]{1,0:T(8,128)(2,1)}, u32[]{:S(2)}, u32[]{:S(2)}) collective-permute-start(bf16[512,512]{1,0:T(8,128)(2,1)S(1)} %copy-done.2), channel_id=1, source_target_pairs={{0,8},{8,0},{16,24},{24,16},{32,40},{40,32},{48,56},{56,48},{64,72... | collective-permute-start | bytes 1572872 | tf_op jit(solution)/shard_map/ppermute | solution.py:22
  164.5 35.6 %all-to-all-start.2 = ((f32[64,8,512]{2,1,0:T(8,128)}), f32[64,8,512]{2,1,0:T(8,128)S(1)}, u32[]{:S(2)}, u32[]{:S(2)}) async-start(f32[64,8,512]{2,1,0:T(8,128)} %copy.25), calls=%async_computation.2 | async-start | bytes 2097152 | tf_op jit(solution)/shard_map/all_to_all | solution.py:106
  170.5 189.0 %reduce-scatter.2.cloned.1.call-start = ((), (), s32[]{:S(2)}) async-start(), calls=%async_computation.11 | async-start | bytes 4718592 | tf_op jit(solution)/shard_map/reduce_scatter | solution.py:83
  175.0 25.2 %copy-start = (bf16[512,512]{1,0:T(8,128)(2,1)S(1)}, bf16[512,512]{1,0:T(8,128)(2,1)}, u32[]{:S(2)}) copy-start(bf16[512,512]{1,0:T(8,128)(2,1)} %param.14) | copy-start | bytes 1572868
  175.0 25.2 %copy-start.1 = (bf16[512,512]{1,0:T(8,128)(2,1)S(1)}, bf16[512,512]{1,0:T(8,128)(2,1)}, u32[]{:S(2)}) copy-start(bf16[512,512]{1,0:T(8,128)(2,1)} %param.13) | copy-start | bytes 1572868
  202.0 83.7 %copy-start.4 = (s32[32]{0:T(128)S(1)}, s32[32]{0:T(128)}, u32[]{:S(2)}) copy-start(s32[32]{0:T(128)} %param.16) | copy-start | bytes 388
  269.3 34.0 %all-to-all-start.5 = ((bf16[64,8,512]{2,1,0:T(8,128)(2,1)}), bf16[64,8,512]{2,1,0:T(8,128)(2,1)S(1)}, u32[]{:S(2)}, u32[]{:S(2)}) async-start(bf16[64,8,512]{2,1,0:T(8,128)(2,1)} %get-tuple-element.9), calls=%async_computation.5 | async-start | bytes 1048576 | tf_op jit(solution)/shard_map/all_to_all | solution.py:112
  353.9 23.3 %all-to-all-start.4 = ((bf16[64,8,512]{2,1,0:T(8,128)(2,1)}), bf16[64,8,512]{2,1,0:T(8,128)(2,1)S(1)}, u32[]{:S(2)}, u32[]{:S(2)}) async-start(bf16[64,8,512]{2,1,0:T(8,128)(2,1)} %get-tuple-element.12), calls=%async_computation.4 | async-start | bytes 1048576 | tf_op jit(solution)/shard_map/all_to_all | solution.py:126
Sparse Core Ops, SparseCore 0:
  11.2 98.0 all-gather.1
  176.1 160.2 reduce-scatter.1
where the time goes:
time: 387 us; the launch traced here: 386 us
  waiting for transfers between devices  171 us (44%)
  blocking collectives  116 us (30%)
  starting transfers between devices  55.8 us (14%)
  between operations  14.9 us (4%)
  local copies, waits for them, and re-layouts  12 us (3%)
  matrix products  8.58 us (2%)
  other arithmetic  8.06 us (2%)
    all_gather x1, waiting for transfers between devices, shards(): lax.all_gather(hidden_acts, 'local', axis=0, tiled=True)  65.6 us
    all_to_all x2, blocking collectives, shards(): lax.all_to_all(shortened(migrated), 'node', split_axis=0, concat_axis=0,...  49 us
    all_to_all x1, blocking collectives, shards(): lax.all_to_all(second_new, 'node', split_axis=0, concat_axis=0, tiled=True)  42 us
    all_to_all x1, waiting for transfers between devices, shards(): lax.all_to_all(grad_part, 'node', split_axis=0, concat_axis=0, tiled=True)  26 us
    all_to_all x1, blocking collectives, shards(): lax.all_to_all(weight_new, 'node', split_axis=0, concat_axis=0, tiled=True)  25.3 us
    all_to_all x1, waiting for transfers between devices, shards(): lax.all_to_all(summed.reshape(-1, col_count), 'node', split_axis=0, conca...  25.2 us
    all_to_all x1, waiting for transfers between devices, shards(): lax.all_to_all(masked, 'local', split_axis=1, concat_axis=0, tiled=True)  18.6 us
    all_to_all x1, starting transfers between devices, shards(): lax.all_to_all(first_new, 'node', split_axis=0, concat_axis=0, tiled=True)  16.3 us
  transfers between devices with their start and end apart: 9, of which 7 were waited for; matrix products, arithmetic and copies ran while one was open for 4% of the time, Pallas kernels for 0%

commit v1 on v0

--- a/solution.py
+++ b/solution.py
@@ -73,8 +73,11 @@
         jnp.concatenate([partner_half, weight], axis=0),
     )
     row_part = columns
+    mix_lines = lambda packet, which_dim: jnp.concatenate(
+        lax.all_to_all(jnp.stack(lax.axis_size("local") * [packet], 0), "local", 0, 0), which_dim
+    )
     grad_whole = lax.dot_general(
-        lax.all_gather(hidden_acts, "local", axis=0, tiled=True),
+        mix_lines(hidden_acts, 0),
         row_part,
         (((0,), (0,)), ((), ())),
         preferred_element_type=jnp.float32,

time: 387 us -> 388 us (level)
  the two profiles are of different devices: /device:TPU:1 before, /device:TPU:5 now
where the time goes in v1:
time: 388 us; the launch traced here: 387 us
  blocking collectives  160 us (41%)
  waiting for transfers between devices  105 us (27%)
  starting transfers between devices  79.6 us (21%)
  between operations  14.9 us (4%)
  local copies, waits for them, and re-layouts  11.7 us (3%)
  other arithmetic  8.46 us (2%)
  matrix products  7.32 us (2%)
    all_to_all x2, blocking collectives, shards(): lax.all_to_all(shortened(migrated), 'node', split_axis=0, concat_axis=0,...  55 us
    all_to_all x1, blocking collectives, shards(): lax.all_to_all(weight_new, 'node', split_axis=0, concat_axis=0, tiled=True)  40.8 us
    all_to_all x1, starting transfers between devices, shards(): lax.all_to_all(grad_part, 'node', split_axis=0, concat_axis=0, tiled=True)  38.4 us
    all_to_all x1, blocking collectives, shards(): lax.all_to_all(second_new, 'node', split_axis=0, concat_axis=0, tiled=True)  35.3 us
    all_to_all x1, blocking collectives, shards(): lax.all_to_all(masked, 'local', split_axis=1, concat_axis=0, tiled=True)  29.1 us
    all_to_all x1, waiting for transfers between devices, shards(): lax.all_to_all(grad_part, 'node', split_axis=0, concat_axis=0, tiled=True)  26 us
    all_to_all x1, waiting for transfers between devices, shards(): lax.all_to_all(summed.reshape(-1, col_count), 'node', split_axis=0, conca...  23.6 us
    all_to_all x1, waiting for transfers between devices, shards(): lax.all_to_all(jnp.stack(lax.axis_size('local') * [packet], 0), 'local',...  20.1 us
  transfers between devices with their start and end apart: 8, of which 6 were waited for; matrix products, arithmetic and copies ran while one was open for 4% of the time, Pallas kernels for 0%

profile of v1, /device:TPU:5, one launch (start us, length us, event | category | flops | bytes accessed | tf_op | source)
XLA Modules:
  0.0 387.0 jit_solution(4430717616407658378)
XLA Ops:
  7.8 1.4 broadcast_select_fusion
  9.9 29.1 %all_to_all.96 = bf16[128,8,512]{0,2,1:T(8,128)(2,1)S(1)} all-to-all(bf16[128,8,512]{0,2,1:T(8,128)(2,1)S(1)} %bitcast.47), channel_id=1, replica_groups=mesh['node'=64,'local'=8] {'local'}, dimensions={1} | all-to-all | bytes 2097152 | tf_op jit(solution)/shard_map/all_to_all | solution.py:67
  39.0 1.6 stack.2
  40.6 5.1 %all-to-all-start.1 = ((bf16[8,128,1024]{2,1,0:T(8,128)(2,1)}), bf16[8,128,1024]{2,1,0:T(8,128)(2,1)S(1)}, u32[]{:S(2)}, u32[]{:S(2)}) async-start(bf16[8,128,1024]{2,1,0:T(8,128)(2,1)} %stack.2), calls=%async_computation.1 | async-start | bytes 4194304 | tf_op jit(solution)/shard_map/all_to_all | solution.py:77
  45.7 20.1 %all-to-all-done.1 = bf16[8,128,1024]{2,1,0:T(8,128)(2,1)S(1)} async-done(((bf16[8,128,1024]{2,1,0:T(8,128)(2,1)}), bf16[8,128,1024]{2,1,0:T(8,128)(2,1)S(1)}, u32[]{:S(2)}, u32[]{:S(2)}) %all-to-all-start.1) | async-done | bytes 2097184 | tf_op jit(solution)/shard_map/all_to_all | solution.py:77
  65.7 1.2 convolution_bitcast_fusion
  67.0 1.3 copy-done
  68.4 12.6 %collective-permute-start = (f32[512,512]{0,1:T(8,128)S(1)}, f32[512,512]{0,1:T(8,128)S(1)}, u32[]{:S(2)}, u32[]{:S(2)}) collective-permute-start(f32[512,512]{0,1:T(8,128)S(1)} %dynamic-slice_bitcast_fusion), channel_id=1, source_target_pairs={{0,8},{8,0},{16,24},{24,16},{32,40},{40,32},{48,56},{56,48},{64,72... | collective-permute-start | bytes 3145736 | tf_op jit(solution)/shard_map/ppermute | solution.py:22
  81.1 2.3 collective-permute-done
  83.3 1.4 bitcast_add_fusion
  84.8 1.3 copy.20
  86.1 38.4 %all-to-all-start.2 = ((f32[64,8,512]{2,1,0:T(8,128)}), f32[64,8,512]{2,1,0:T(8,128)S(1)}, u32[]{:S(2)}, u32[]{:S(2)}) async-start(f32[64,8,512]{2,1,0:T(8,128)} %bitcast.7), calls=%async_computation.2 | async-start | bytes 2097152 | tf_op jit(solution)/shard_map/all_to_all | solution.py:106
  124.5 2.4 collective-permute-start.1
  127.0 26.0 %all-to-all-done.2 = f32[64,8,512]{2,1,0:T(8,128)S(1)} async-done(((f32[64,8,512]{2,1,0:T(8,128)}), f32[64,8,512]{2,1,0:T(8,128)S(1)}, u32[]{:S(2)}, u32[]{:S(2)}) %all-to-all-start.2) | async-done | bytes 1048608 | tf_op jit(solution)/shard_map/all_to_all | solution.py:106
  153.0 1.3 fusion.11
  154.3 1.6 copy.22
  155.9 6.0 %all-to-all-start.3 = ((f32[64,8,512]{2,1,0:T(8,128)}), f32[64,8,512]{2,1,0:T(8,128)S(1)}, u32[]{:S(2)}, u32[]{:S(2)}) async-start(f32[64,8,512]{2,1,0:T(8,128)} %copy.22), calls=%async_computation.3 | async-start | bytes 2097152 | tf_op jit(solution)/shard_map/all_to_all | solution.py:109
  162.5 4.8 %fusion.4 = f32[1024,1024]{1,0:T(8,128)} fusion(bf16[1024,512]{1,0:T(8,128)(2,1)S(1)} %bitcast.51, bf16[512,512]{1,0:T(8,128)(2,1)} %collective-permute-done.1, bf16[512,512]{1,0:T(8,128)(2,1)} %param.12, pred[]{:T(512)S(6)} %eq.42), kind=kOutput, calls=%fused_computation.12 | convolution fusion | flops 1078460416 | bytes 6291457 | tf_op jit(solution)/shard_map/dot_general | solution.py:87
  167.3 23.6 %all-to-all-done.3 = f32[64,8,512]{2,1,0:T(8,128)S(1)} async-done(((f32[64,8,512]{2,1,0:T(8,128)}), f32[64,8,512]{2,1,0:T(8,128)S(1)}, u32[]{:S(2)}, u32[]{:S(2)}) %all-to-all-start.3) | async-done | bytes 1048608 | tf_op jit(solution)/shard_map/all_to_all | solution.py:109
  190.9 2.8 fusion.16
  193.8 35.3 %all_to_all.97 = bf16[64,8,512]{2,1,0:T(8,128)(2,1)S(1)} all-to-all(bf16[64,8,512]{2,1,0:T(8,128)(2,1)S(1)} %get-tuple-element.7), channel_id=1, replica_groups=mesh['node'=64,'local'=8] {'node'}, dimensions={0} | all-to-all | bytes 1048576 | tf_op jit(solution)/shard_map/all_to_all | solution.py:116
  229.0 40.8 %all_to_all.98 = bf16[64,8,512]{2,1,0:T(8,128)(2,1)S(1)} all-to-all(bf16[64,8,512]{2,1,0:T(8,128)(2,1)S(1)} %get-tuple-element.8), channel_id=1, replica_groups=mesh['node'=64,'local'=8] {'node'}, dimensions={0} | all-to-all | bytes 1048576 | tf_op jit(solution)/shard_map/all_to_all | solution.py:114
  269.8 9.6 %all-to-all-start.6 = ((bf16[64,8,512]{2,1,0:T(8,128)(2,1)}), bf16[64,8,512]{2,1,0:T(8,128)(2,1)S(1)}, u32[]{:S(2)}, u32[]{:S(2)}) async-start(bf16[64,8,512]{2,1,0:T(8,128)(2,1)} %get-tuple-element.9), calls=%async_computation.6 | async-start | bytes 1048576 | tf_op jit(solution)/shard_map/all_to_all | solution.py:115
  280.9 17.0 %all-to-all-done.6 = bf16[64,8,512]{2,1,0:T(8,128)(2,1)S(1)} async-done(((bf16[64,8,512]{2,1,0:T(8,128)(2,1)}), bf16[64,8,512]{2,1,0:T(8,128)(2,1)S(1)}, u32[]{:S(2)}, u32[]{:S(2)}) %all-to-all-start.6) | async-done | bytes 524320 | tf_op jit(solution)/shard_map/all_to_all | solution.py:115
  298.5 1.0 broadcast_select_fusion.1
  299.5 32.0 %all_to_all.99 = bf16[64,8,512]{2,1,0:T(8,128)(2,1)S(1)} all-to-all(bf16[64,8,512]{2,1,0:T(8,128)(2,1)S(1)} %get-tuple-element.10), channel_id=1, replica_groups=mesh['node'=64,'local'=8] {'node'}, dimensions={0} | all-to-all | bytes 1048576 | tf_op jit(solution)/shard_map/all_to_all | solution.py:129
  331.4 23.1 %all_to_all.100 = bf16[64,8,512]{2,1,0:T(8,128)(2,1)S(1)} all-to-all(bf16[64,8,512]{2,1,0:T(8,128)(2,1)S(1)} %get-tuple-element.11), channel_id=1, replica_groups=mesh['node'=64,'local'=8] {'node'}, dimensions={0} | all-to-all | bytes 1048576 | tf_op jit(solution)/shard_map/all_to_all | solution.py:129
  354.5 5.6 %all-to-all-start.5 = ((bf16[64,8,512]{2,1,0:T(8,128)(2,1)}), bf16[64,8,512]{2,1,0:T(8,128)(2,1)S(1)}, u32[]{:S(2)}, u32[]{:S(2)}) async-start(bf16[64,8,512]{2,1,0:T(8,128)(2,1)} %get-tuple-element.12), calls=%async_computation.5 | async-start | bytes 1048576 | tf_op jit(solution)/shard_map/all_to_all | solution.py:129
  360.1 1.8 convert_element_type.28
  361.9 15.9 %all-to-all-done.5 = bf16[64,8,512]{2,1,0:T(8,128)(2,1)S(1)} async-done(((bf16[64,8,512]{2,1,0:T(8,128)(2,1)}), bf16[64,8,512]{2,1,0:T(8,128)(2,1)S(1)}, u32[]{:S(2)}, u32[]{:S(2)}) %all-to-all-start.5) | async-done | bytes 524320 | tf_op jit(solution)/shard_map/all_to_all | solution.py:129
  377.8 0.8 copy.30
  379.4 0.8 copy.32
  (31 shorter events, 4.3 us)
Async XLA Ops:
  9.2 29.8 %copy-start.3 = (bf16[128,1024]{1,0:T(8,128)(2,1)S(1)}, bf16[128,1024]{1,0:T(8,128)(2,1)}, u32[]{:S(2)}) copy-start(bf16[128,1024]{1,0:T(8,128)(2,1)} %param.10) | copy-start | bytes 786436
  40.6 25.2 %all-to-all-start.1 = ((bf16[8,128,1024]{2,1,0:T(8,128)(2,1)}), bf16[8,128,1024]{2,1,0:T(8,128)(2,1)S(1)}, u32[]{:S(2)}, u32[]{:S(2)}) async-start(bf16[8,128,1024]{2,1,0:T(8,128)(2,1)} %stack.2), calls=%async_computation.1 | async-start | bytes 4194304 | tf_op jit(solution)/shard_map/all_to_all | solution.py:77
  67.0 1.3 copy-start
  68.4 14.9 %collective-permute-start = (f32[512,512]{0,1:T(8,128)S(1)}, f32[512,512]{0,1:T(8,128)S(1)}, u32[]{:S(2)}, u32[]{:S(2)}) collective-permute-start(f32[512,512]{0,1:T(8,128)S(1)} %dynamic-slice_bitcast_fusion), channel_id=1, source_target_pairs={{0,8},{8,0},{16,24},{24,16},{32,40},{40,32},{48,56},{56,48},{64,72... | collective-permute-start | bytes 3145736 | tf_op jit(solution)/shard_map/ppermute | solution.py:22
  84.7 42.1 %copy-start.4 = (s32[32]{0:T(128)S(1)}, s32[32]{0:T(128)}, u32[]{:S(2)}) copy-start(s32[32]{0:T(128)} %param.15) | copy-start | bytes 388
  86.1 66.9 %all-to-all-start.2 = ((f32[64,8,512]{2,1,0:T(8,128)}), f32[64,8,512]{2,1,0:T(8,128)S(1)}, u32[]{:S(2)}, u32[]{:S(2)}) async-start(f32[64,8,512]{2,1,0:T(8,128)} %bitcast.7), calls=%async_computation.2 | async-start | bytes 2097152 | tf_op jit(solution)/shard_map/all_to_all | solution.py:106
  124.5 38.0 %collective-permute-start.1 = (bf16[512,512]{1,0:T(8,128)(2,1)}, bf16[512,512]{1,0:T(8,128)(2,1)}, u32[]{:S(2)}, u32[]{:S(2)}) collective-permute-start(bf16[512,512]{1,0:T(8,128)(2,1)} %param.12), channel_id=1, source_target_pairs={{0,8},{8,0},{16,24},{24,16},{32,40},{40,32},{48,56},{56,48},{64,72... | collective-permute-start | bytes 1572872 | tf_op jit(solution)/shard_map/ppermute | solution.py:22
  155.9 35.0 %all-to-all-start.3 = ((f32[64,8,512]{2,1,0:T(8,128)}), f32[64,8,512]{2,1,0:T(8,128)S(1)}, u32[]{:S(2)}, u32[]{:S(2)}) async-start(f32[64,8,512]{2,1,0:T(8,128)} %copy.22), calls=%async_computation.3 | async-start | bytes 2097152 | tf_op jit(solution)/shard_map/all_to_all | solution.py:109
  161.9 198.2 %reduce-scatter.2.cloned.1.call-start = ((), (), s32[]{:S(2)}) async-start(), calls=%async_computation.11 | async-start | bytes 4718592 | tf_op jit(solution)/shard_map/reduce_scatter | solution.py:86
  167.2 23.7 %copy-start.1 = (bf16[512,512]{1,0:T(8,128)(2,1)S(1)}, bf16[512,512]{1,0:T(8,128)(2,1)}, u32[]{:S(2)}) copy-start(bf16[512,512]{1,0:T(8,128)(2,1)} %param.14) | copy-start | bytes 1572868
  167.3 23.7 %copy-start.2 = (bf16[512,512]{1,0:T(8,128)(2,1)S(1)}, bf16[512,512]{1,0:T(8,128)(2,1)}, u32[]{:S(2)}) copy-start(bf16[512,512]{1,0:T(8,128)(2,1)} %param.13) | copy-start | bytes 1572868
  193.8 85.7 %copy-start.5 = (s32[32]{0:T(128)S(1)}, s32[32]{0:T(128)}, u32[]{:S(2)}) copy-start(s32[32]{0:T(128)} %param.16) | copy-start | bytes 388
  269.8 28.0 %all-to-all-start.6 = ((bf16[64,8,512]{2,1,0:T(8,128)(2,1)}), bf16[64,8,512]{2,1,0:T(8,128)(2,1)S(1)}, u32[]{:S(2)}, u32[]{:S(2)}) async-start(bf16[64,8,512]{2,1,0:T(8,128)(2,1)} %get-tuple-element.9), calls=%async_computation.6 | async-start | bytes 1048576 | tf_op jit(solution)/shard_map/all_to_all | solution.py:115
  354.5 23.3 %all-to-all-start.5 = ((bf16[64,8,512]{2,1,0:T(8,128)(2,1)}), bf16[64,8,512]{2,1,0:T(8,128)(2,1)S(1)}, u32[]{:S(2)}, u32[]{:S(2)}) async-start(bf16[64,8,512]{2,1,0:T(8,128)(2,1)} %get-tuple-element.12), calls=%async_computation.5 | async-start | bytes 1048576 | tf_op jit(solution)/shard_map/all_to_all | solution.py:129
Sparse Core Ops, SparseCore 0:
  167.4 155.1 reduce-scatter.1
